TPU v7x, 128 devices: a whole 4x4x4 slice. The times are simulated.
128 devices in a mesh: img: 8 (over y, x_lo), ori: 16 (over z, x_hi, core).
Axes of the slice: x: 4 (x_hi: 2, x_lo: 2; x = x_hi * 2 + x_lo), y: 4, z: 4, core: 2. Of those that a mesh axis runs over, the one named last changes fastest.
Arguments:
- images: bfloat16 [3072, 16384], P('img'), may hold values from -16 to 16
- noise_precision: float32 [3072], P('img'), as said below
- prior_weight: float32 [128], replicated, may hold values from 0.25 to 4
- bead_coords: float32 [128, 3, 3000], replicated, may hold values from -96 to 96
- euler_angles: float32 [3, 64], P(None, 'ori'), may hold values from -3.140625 to 3.140625
- template_conf: int32 [6144], P('ori'), may hold values from 0 to 127, as said below
- template_orient: int32 [6144], P('ori'), may hold values from 0 to 3
Outputs:
- new_weights: float32 [128], replicated
- log_evidence: float32 [3072], P('img')
Inputs may be any that keep to these rules, and one draw needn't show every extreme that they name: `template_conf`: every conformation is rendered in one template or more. `noise_precision`: each value lies between 80 / 128 and 160 / 128.
All inputs are finite; a program needn't handle non-finite values.
Results may differ from a plain program's by a relative error of at most 0.0025.
The roundings to bfloat16 on the way count: a program that leaves them out, or rounds other values in their place, can miss the bound.
Values may be sent and summed in bfloat16 or wider, within the bound.
A program may use at most 128 MiB of HBM per device.

v0:
```python
import jax
import jax.numpy as jnp
from jax import lax
from jax.sharding import PartitionSpec as P

GRID = 128
K = 128
TPL_DEV = 48


BLOB_SIGMA = 1.5


def rotation_rows(angles):
    ca, sa = (jnp.cos(angles[0]), jnp.sin(angles[0]))
    cb, sb = (jnp.cos(angles[1]), jnp.sin(angles[1]))
    cg, sg = (jnp.cos(angles[2]), jnp.sin(angles[2]))
    first = (ca * cb * cg - sa * sg, -ca * cb * sg - sa * cg, ca * sb)
    second = (sa * cb * cg + ca * sg, -sa * cb * sg + ca * cg, sa * sb)
    return (first, second)


def render(chosen, angles):
    first, second = rotation_rows(angles)
    centre = (GRID - 1) / 2.0
    coord_u = (
        first[0][:, None] * chosen[:, 0]
        + first[1][:, None] * chosen[:, 1]
        + first[2][:, None] * chosen[:, 2]
        + centre
    )
    coord_v = (
        second[0][:, None] * chosen[:, 0]
        + second[1][:, None] * chosen[:, 1]
        + second[2][:, None] * chosen[:, 2]
        + centre
    )
    pixels = jnp.arange(GRID, dtype=jnp.float32)
    factor = 0.5 / (BLOB_SIGMA * BLOB_SIGMA)
    gauss_u = jnp.exp(-jnp.square(coord_u[:, :, None] - pixels) * factor).astype(jnp.bfloat16)
    gauss_v = jnp.exp(-jnp.square(coord_v[:, :, None] - pixels) * factor).astype(jnp.bfloat16)
    raw = jnp.einsum("nbp,nbq->npq", gauss_u, gauss_v, preferred_element_type=jnp.float32)
    raw = raw.reshape(raw.shape[0], GRID * GRID)
    centred = raw - jnp.mean(raw, axis=1, keepdims=True)
    spread = jnp.mean(centred * centred, axis=1, keepdims=True)
    return (centred * lax.rsqrt(spread + 1e-05)).astype(jnp.bfloat16)


def local(
    images, noise_precision, prior_weight, bead_coords, euler_angles, template_conf, template_orient
):
    img_rank = lax.axis_index("img")
    mine_conf = lax.dynamic_slice_in_dim(template_conf, img_rank * TPL_DEV, TPL_DEV)
    mine_orient = lax.dynamic_slice_in_dim(template_orient, img_rank * TPL_DEV, TPL_DEV)
    orient_table = (
        mine_orient[:, None] == jnp.arange(euler_angles.shape[1], dtype=jnp.int32)[None, :]
    ).astype(jnp.float32)
    angles = jnp.dot(euler_angles, orient_table.T, precision=lax.Precision.HIGHEST)
    groups = TPL_DEV // 4
    conf_groups = mine_conf.reshape(groups, 4)
    angle_groups = angles.reshape(3, groups, 4).transpose(1, 0, 2)
    rendered = lax.map(
        lambda item: render(bead_coords[item[0]], item[1]), (conf_groups, angle_groups)
    )
    rendered = rendered.reshape(TPL_DEV, GRID * GRID)
    log_prior = jnp.log(prior_weight) - jnp.log(jnp.sum(prior_weight))
    conf_onehot = (template_conf[:, None] == jnp.arange(K, dtype=jnp.int32)[None, :]).astype(
        jnp.float32
    )
    bias_column = jnp.dot(conf_onehot, log_prior, precision=lax.Precision.HIGHEST)
    image_total = images.shape[0] * lax.axis_size("img")
    raw = lax.dot_general(
        images,
        lax.all_gather(rendered, "img", axis=0, tiled=True),
        (((1,), (1,)), ((), ())),
        preferred_element_type=jnp.float32,
    )
    logits = noise_precision[:, None] * raw + bias_column[None, :]
    row_top = jnp.max(logits, axis=1)
    row_sum = jnp.sum(jnp.exp(logits - row_top[:, None]), axis=1)
    global_top = lax.pmax(row_top, "ori")
    row_sum = lax.psum(row_sum * jnp.exp(row_top - global_top), "ori")
    row_top = global_top
    evidence = row_top + jnp.log(row_sum)
    column_mass = jnp.sum(jnp.exp(logits - evidence[:, None]), axis=0)
    conf_mass = jnp.dot(column_mass, conf_onehot, precision=lax.Precision.HIGHEST)
    totals = lax.psum(conf_mass, ("img", "ori"))
    new_weights = K * totals / image_total
    return (new_weights, evidence)


def solution(mesh):
    placed = (P("img", None), P("img"), P(), P(), P(None, "ori"), P("ori"), P("ori"))
    return jax.shard_map(
        local, mesh=mesh, in_specs=placed, out_specs=(P(), P("img")), check_vma=False
    )
```

profile of v0, /device:TPU:1, one launch (start us, length us, event | category | flops | bytes accessed | tf_op | source)
XLA Modules:
  0.0 552.6 jit_solution(13335791167175924144)
XLA Ops:
  7.2 0.8 dynamic_slice.14
  8.0 0.2 convolution_bitcast_fusion
  8.3 0.8 dynamic_slice.15
  9.1 7.3 %copy.15 = f32[128,3,3000]{2,1,0:T(4,128)} copy(f32[128,3,3000]{0,2,1:T(8,128)} %param.12) | data formatting | bytes 9216000 | tf_op jit(solution)/shard_map/while | solution.py:62
  16.5 123.7 %while.10 = (s32[]{:T(128)}, bf16[12,4,16384]{2,1,0:T(4,128)(2,1)S(1)}, f32[12,3,4]{2,0,1:T(8,128)S(1)}, s32[12,4]{1,0:T(8,128)S(1)}, f32[128,3,3000]{2,1,0:T(4,128)}, /*index=5*/s32[]{:T(128)}, s32[]{:T(128)}, s32[]{}, s32[]{}) while((s32[]{:T(128)}, bf16[12,4,16384]{2,1,0:T(4,128)(2,1)S(1)}, f32[12,3,4]{2,0,1:T(8,128)S(1)}, ...), condition=%wide.region_3.4_spmd, body=%wide.region_0.3_spmd.sunk | while | flops 409179872 | bytes 2359649 | solution.py:62
  16.7 3.4 gather_fusion
  20.4 5.9 %fusion.61 = (f32[4]{0:T(128)S(1)}, f32[4,128,128]{2,1,0:T(8,128)S(1)}) fusion(f32[4,3000]{1,0:T(4,128)S(1)} %get-tuple-element.130, f32[4,3000]{1,0:T(4,128)S(1)} %get-tuple-element.131), kind=kOutput, calls=%fused_computation.80.clone.1 | convolution fusion | flops 408641536 | bytes 358160 | tf_op jit(solution)/shard_map/while/body/eval_jaxpr/nbp,nbq->npq/dot_general | solution.py:42
  26.3 0.2 multiply_reduce_fusion.2
  26.6 0.2 fusion.62
  27.0 3.4 gather_fusion
  30.7 5.9 %fusion.61 = (f32[4]{0:T(128)S(1)}, f32[4,128,128]{2,1,0:T(8,128)S(1)}) fusion(f32[4,3000]{1,0:T(4,128)S(1)} %get-tuple-element.130, f32[4,3000]{1,0:T(4,128)S(1)} %get-tuple-element.131), kind=kOutput, calls=%fused_computation.80.clone.1 | convolution fusion | flops 408641536 | bytes 358160 | tf_op jit(solution)/shard_map/while/body/eval_jaxpr/nbp,nbq->npq/dot_general | solution.py:42
  36.6 0.2 multiply_reduce_fusion.2
  36.9 0.2 fusion.62
  37.3 3.4 gather_fusion
  41.0 5.9 %fusion.61 = (f32[4]{0:T(128)S(1)}, f32[4,128,128]{2,1,0:T(8,128)S(1)}) fusion(f32[4,3000]{1,0:T(4,128)S(1)} %get-tuple-element.130, f32[4,3000]{1,0:T(4,128)S(1)} %get-tuple-element.131), kind=kOutput, calls=%fused_computation.80.clone.1 | convolution fusion | flops 408641536 | bytes 358160 | tf_op jit(solution)/shard_map/while/body/eval_jaxpr/nbp,nbq->npq/dot_general | solution.py:42
  46.9 0.2 multiply_reduce_fusion.2
  47.3 0.2 fusion.62
  47.6 3.4 gather_fusion
  51.3 5.9 %fusion.61 = (f32[4]{0:T(128)S(1)}, f32[4,128,128]{2,1,0:T(8,128)S(1)}) fusion(f32[4,3000]{1,0:T(4,128)S(1)} %get-tuple-element.130, f32[4,3000]{1,0:T(4,128)S(1)} %get-tuple-element.131), kind=kOutput, calls=%fused_computation.80.clone.1 | convolution fusion | flops 408641536 | bytes 358160 | tf_op jit(solution)/shard_map/while/body/eval_jaxpr/nbp,nbq->npq/dot_general | solution.py:42
  57.2 0.2 multiply_reduce_fusion.2
  57.6 0.2 fusion.62
  57.9 3.4 gather_fusion
  61.6 5.9 %fusion.61 = (f32[4]{0:T(128)S(1)}, f32[4,128,128]{2,1,0:T(8,128)S(1)}) fusion(f32[4,3000]{1,0:T(4,128)S(1)} %get-tuple-element.130, f32[4,3000]{1,0:T(4,128)S(1)} %get-tuple-element.131), kind=kOutput, calls=%fused_computation.80.clone.1 | convolution fusion | flops 408641536 | bytes 358160 | tf_op jit(solution)/shard_map/while/body/eval_jaxpr/nbp,nbq->npq/dot_general | solution.py:42
  67.5 0.2 multiply_reduce_fusion.2
  67.9 0.2 fusion.62
  68.2 3.4 gather_fusion
  71.9 5.9 %fusion.61 = (f32[4]{0:T(128)S(1)}, f32[4,128,128]{2,1,0:T(8,128)S(1)}) fusion(f32[4,3000]{1,0:T(4,128)S(1)} %get-tuple-element.130, f32[4,3000]{1,0:T(4,128)S(1)} %get-tuple-element.131), kind=kOutput, calls=%fused_computation.80.clone.1 | convolution fusion | flops 408641536 | bytes 358160 | tf_op jit(solution)/shard_map/while/body/eval_jaxpr/nbp,nbq->npq/dot_general | solution.py:42
  77.8 0.2 multiply_reduce_fusion.2
  78.2 0.2 fusion.62
  78.5 3.4 gather_fusion
  82.2 5.9 %fusion.61 = (f32[4]{0:T(128)S(1)}, f32[4,128,128]{2,1,0:T(8,128)S(1)}) fusion(f32[4,3000]{1,0:T(4,128)S(1)} %get-tuple-element.130, f32[4,3000]{1,0:T(4,128)S(1)} %get-tuple-element.131), kind=kOutput, calls=%fused_computation.80.clone.1 | convolution fusion | flops 408641536 | bytes 358160 | tf_op jit(solution)/shard_map/while/body/eval_jaxpr/nbp,nbq->npq/dot_general | solution.py:42
  88.1 0.2 multiply_reduce_fusion.2
  88.5 0.2 fusion.62
  88.8 3.4 gather_fusion
  92.5 5.9 %fusion.61 = (f32[4]{0:T(128)S(1)}, f32[4,128,128]{2,1,0:T(8,128)S(1)}) fusion(f32[4,3000]{1,0:T(4,128)S(1)} %get-tuple-element.130, f32[4,3000]{1,0:T(4,128)S(1)} %get-tuple-element.131), kind=kOutput, calls=%fused_computation.80.clone.1 | convolution fusion | flops 408641536 | bytes 358160 | tf_op jit(solution)/shard_map/while/body/eval_jaxpr/nbp,nbq->npq/dot_general | solution.py:42
  98.5 0.2 multiply_reduce_fusion.2
  98.8 0.2 fusion.62
  99.1 3.4 gather_fusion
  102.8 5.9 %fusion.61 = (f32[4]{0:T(128)S(1)}, f32[4,128,128]{2,1,0:T(8,128)S(1)}) fusion(f32[4,3000]{1,0:T(4,128)S(1)} %get-tuple-element.130, f32[4,3000]{1,0:T(4,128)S(1)} %get-tuple-element.131), kind=kOutput, calls=%fused_computation.80.clone.1 | convolution fusion | flops 408641536 | bytes 358160 | tf_op jit(solution)/shard_map/while/body/eval_jaxpr/nbp,nbq->npq/dot_general | solution.py:42
  108.8 0.2 multiply_reduce_fusion.2
  109.1 0.2 fusion.62
  109.4 3.4 gather_fusion
  113.1 5.9 %fusion.61 = (f32[4]{0:T(128)S(1)}, f32[4,128,128]{2,1,0:T(8,128)S(1)}) fusion(f32[4,3000]{1,0:T(4,128)S(1)} %get-tuple-element.130, f32[4,3000]{1,0:T(4,128)S(1)} %get-tuple-element.131), kind=kOutput, calls=%fused_computation.80.clone.1 | convolution fusion | flops 408641536 | bytes 358160 | tf_op jit(solution)/shard_map/while/body/eval_jaxpr/nbp,nbq->npq/dot_general | solution.py:42
  119.1 0.2 multiply_reduce_fusion.2
  119.4 0.2 fusion.62
  119.7 3.4 gather_fusion
  123.4 5.9 %fusion.61 = (f32[4]{0:T(128)S(1)}, f32[4,128,128]{2,1,0:T(8,128)S(1)}) fusion(f32[4,3000]{1,0:T(4,128)S(1)} %get-tuple-element.130, f32[4,3000]{1,0:T(4,128)S(1)} %get-tuple-element.131), kind=kOutput, calls=%fused_computation.80.clone.1 | convolution fusion | flops 408641536 | bytes 358160 | tf_op jit(solution)/shard_map/while/body/eval_jaxpr/nbp,nbq->npq/dot_general | solution.py:42
  129.4 0.2 multiply_reduce_fusion.2
  129.7 0.2 fusion.62
  130.0 3.4 gather_fusion
  133.7 5.9 %fusion.61 = (f32[4]{0:T(128)S(1)}, f32[4,128,128]{2,1,0:T(8,128)S(1)}) fusion(f32[4,3000]{1,0:T(4,128)S(1)} %get-tuple-element.130, f32[4,3000]{1,0:T(4,128)S(1)} %get-tuple-element.131), kind=kOutput, calls=%fused_computation.80.clone.1 | convolution fusion | flops 408641536 | bytes 358160 | tf_op jit(solution)/shard_map/while/body/eval_jaxpr/nbp,nbq->npq/dot_general | solution.py:42
  139.7 0.2 multiply_reduce_fusion.2
  140.0 0.2 fusion.62
  140.2 1.9 reshape.351
  142.1 0.6 reduce_sum.45
  143.4 0.3 convolution_reduce_fusion
  143.7 248.5 %all-gather.2.cloned.1.call-done = bf16[384,16384]{1,0:T(8,128)(2,1)} async-done(((bf16[48,16384]{1,0:T(8,128)(2,1)}), bf16[384,16384]{1,0:T(8,128)(2,1)}) %all-gather.2.cloned.1.call-update) | async-done | bytes 12582928 | tf_op jit(solution)/shard_map/all_gather | solution.py:74
  392.2 17.4 %fusion.44 = (f32[384]{0:T(512)S(1)}, f32[384,384]{1,0:T(8,128)S(1)}) fusion(f32[384]{0:T(512)S(1)} %convolution_reduce_fusion, bf16[384,16384]{1,0:T(8,128)(2,1)} %all-gather.2.cloned.1.call-done, bf16[384,16384]{1,0:T(8,128)(2,1)} %param.9, f32[384]{0:T(512)S(1)} %copy-done.2), kind=kOutput, calls=%fused_computation.81 | convolution fusion | flops 4832280064 | bytes 25760256 | tf_op jit(solution)/shard_map/dot_general | solution.py:72
  409.6 33.4 %pmax.7 = f32[384]{0:T(512)S(1)} all-reduce(f32[384]{0:T(512)S(1)} %get-tuple-element.65), channel_id=1, replica_groups=mesh['img'=8,'ori'=16] {'ori'}, use_global_device_ids=true, to_apply=%region_6.7 | all-reduce | flops 384 | bytes 3072 | tf_op jit(solution)/shard_map/pmax | solution.py:81
  443.1 37.5 %psum.14 = f32[384]{0:T(512)S(1)} all-reduce(f32[384]{0:T(512)S(1)} %exponential_multiply_fusion), channel_id=1, replica_groups=mesh['img'=8,'ori'=16] {'ori'}, use_global_device_ids=true, to_apply=%region_8.9 | all-reduce | flops 384 | bytes 3072 | tf_op jit(solution)/shard_map/psum | solution.py:82
  480.6 0.2 exponential_reduce_fusion
  480.7 0.3 convolution_bitcast_fusion.1
  481.0 64.2 %psum.15 = f32[128]{0:T(128)S(1)} all-reduce(f32[128]{0:T(128)S(1)} %convolution_bitcast_fusion.1), channel_id=1, replica_groups=mesh['img'=8,'ori'=16] {'img','ori'}, use_global_device_ids=true, to_apply=%region_10.11 | all-reduce | flops 128 | bytes 1024 | tf_op jit(solution)/shard_map/psum | solution.py:87
  545.2 0.5 broadcast_multiply_fusion.1
  (127 shorter events, 6.3 us)
Async XLA Ops:
  7.2 0.8 copy-start
  7.2 385.0 %all-gather.2.cloned.1.call-start = ((), (), s32[]{:S(2)}) async-start(), calls=%async_computation | async-start | bytes 14155776 | tf_op jit(solution)/shard_map/all_gather | solution.py:74
  16.5 125.6 %copy-start.4 = (f32[128]{0:T(128)S(1)}, f32[128]{0:T(128)}, u32[]{:S(2)}) copy-start(f32[128]{0:T(128)} %param.11) | copy-start | bytes 1540
  16.5 126.9 %copy-start.3 = (s32[384]{0:T(512)S(1)}, s32[384]{0:T(512)}, u32[]{:S(2)}) copy-start(s32[384]{0:T(512)} %param.14) | copy-start | bytes 4612
  16.5 375.7 %copy-start.2 = (f32[384]{0:T(512)S(1)}, f32[384]{0:T(512)}, u32[]{:S(2)}) copy-start(f32[384]{0:T(512)} %param.10) | copy-start | bytes 4612
  480.5 65.2 %copy-start.1 = (f32[384]{0:T(512)}, f32[384]{0:T(512)S(1)}, u32[]{:S(2)}) copy-start(f32[384]{0:T(512)S(1)} %log_add_fusion) | copy-start | bytes 4612
Sparse Core Ops, SparseCore 0:
  142.2 249.9 all-gather.1
where the time goes:
time: 553 us
  waiting for transfers between devices  248 us (45%)
  blocking collectives  135 us (24%)
  matrix products  89.4 us (16%)
  local copies, waits for them, and re-layouts  55 us (10%)
  between operations  14.8 us (3%)
  other arithmetic  9.07 us (2%)
    all_gather x1, waiting for transfers between devices, local(): lax.all_gather(rendered, 'img', axis=0, tiled=True)  248 us
    dot_general x12, matrix products, render(): jnp.einsum('nbp,nbq->npq', gauss_u, gauss_v, preferred_element_type=jnp.f...  71.3 us
    psum x1, blocking collectives, local(): totals = lax.psum(conf_mass, ('img', 'ori'))  64.2 us
    gather x12, local copies, waits for them, and re-layouts, local(): bead_coords[item[0]]  41.4 us
    psum x1, blocking collectives, local(): row_sum = lax.psum(row_sum * jnp.exp(row_top - global_top), 'ori')  37.5 us
    pmax x1, blocking collectives, local(): global_top = lax.pmax(row_top, 'ori')  33.4 us
    dot_general x1, matrix products, local(): lax.dot_general(images, lax.all_gather(rendered, 'img', axis=0, tiled=Tru...  17.4 us
  transfers between devices with their start and end apart: 1, of which 1 were waited for; matrix products, arithmetic and copies ran while one was open for 0% of the time, Pallas kernels for 0%

commit v1 on v0

v1 whole, which is shorter than its diff:
```python
import functools
import math

import jax
import jax.numpy as jnp
from jax import lax
from jax.experimental import pallas as pl
from jax.experimental.pallas import tpu as pltpu
from jax.sharding import PartitionSpec as P

GRID = 128
PIX = GRID * GRID
K = 128
BEADS = 3000
BPAD = 3072
TPL_DEV = 48
N_IMG = 8
N_ORI = 16
IMG_DEV = 384
GROUP = 16
NGROUP = TPL_DEV // GROUP
BLOB_SIGMA = 1.5
SCALE = -0.5 / (BLOB_SIGMA * BLOB_SIGMA) * math.log2(math.e)
MESH = pl.DeviceIdType.MESH
TRANS = (((1,), (1,)), ((), ()))
HIGH = lax.Precision.HIGHEST
CHUNK = 512
SCORE_CHUNK = 2048

LB = 72 * 128
LBH = 36 * 128
LC = PIX - LB
LCH = LC // 2
FULL_B = (0, LB)
B0 = (0, LBH)
B1 = (LBH, LB - LBH)
FULL_C = (LB, LC)
C0 = (LB, LCH)
C1 = (LB + LCH, LC - LCH)

N_KIND = 18


def rotation_rows(angles):
    ca, sa = (jnp.cos(angles[0]), jnp.sin(angles[0]))
    cb, sb = (jnp.cos(angles[1]), jnp.sin(angles[1]))
    cg, sg = (jnp.cos(angles[2]), jnp.sin(angles[2]))
    first = (ca * cb * cg - sa * sg, -ca * cb * sg - sa * cg, ca * sb)
    second = (sa * cb * cg + ca * sg, -sa * cb * sg + ca * cg, sa * sb)
    return jnp.stack(first + second)


def gauss(row, pix):
    d = row - pix
    return jnp.exp2((d * d) * SCALE).astype(jnp.bfloat16)


def kernel(
    images, prec, prior, beads, coef, conf, orient,
    out_w, out_e,
    img_s, tpl, beads_s, u_s, v_s, raw, lt, confb, orib, stat, mass_a, mass_b,
    in_sem, send_sem, recv_sem, ssend, srecv, asend, arecv, bsend, brecv,
):
    r = lax.axis_index("img")
    o = lax.axis_index("ori")
    part = r + 1 - 2 * (r % 2)
    up = (r + 2) % N_IMG
    down = (r + 6) % N_IMG
    up_part = (part + 2) % N_IMG
    down_part = (part + 6) % N_IMG
    far = (r + 4) % N_IMG

    barrier = pltpu.get_barrier_semaphore()
    for j in range(1, N_IMG):
        pl.semaphore_signal(barrier, inc=1, device_id=((r + j) % N_IMG, o), device_id_type=MESH)
    for j in range(1, N_ORI):
        pl.semaphore_signal(barrier, inc=1, device_id=(r, (o + j) % N_ORI), device_id_type=MESH)

    bead_copies = [
        pltpu.make_async_copy(beads.at[c], beads_s.at[c, pl.ds(0, BEADS)], in_sem.at[c]) for c in range(3)
    ]
    for copy in bead_copies:
        copy.start()
    image_copy = pltpu.make_async_copy(images, img_s, in_sem.at[3])
    image_copy.start()

    confb[...] = jnp.broadcast_to(conf[...].astype(jnp.float32), (GRID, TPL_DEV * N_IMG)).T
    orib[...] = jnp.broadcast_to(orient[...].astype(jnp.float32), (GRID, TPL_DEV * N_IMG)).T
    mine = pl.ds(pl.multiple_of(r * TPL_DEV, GROUP), TPL_DEV)
    lane = lax.broadcasted_iota(jnp.int32, (TPL_DEV, K), 1).astype(jnp.float32)
    onehot = (confb[mine, :] == lane).astype(jnp.float32)
    own_orient = orib[mine, :]
    coefs = []
    for c in range(6):
        value = jnp.full((TPL_DEV, K), coef[c, 3], jnp.float32)
        for q in (2, 1, 0):
            value = jnp.where(own_orient == float(q), coef[c, q], value)
        coefs.append(jnp.concatenate([value] * (CHUNK // K), axis=1))
    for c in range(3):
        beads_s[c, BEADS:BPAD, :] = jnp.zeros((BPAD - BEADS, K), jnp.float32)
    for copy in bead_copies:
        copy.wait()
    centre = (GRID - 1) / 2.0

    def place(c, carry):
        rows = pl.ds(pl.multiple_of(c * CHUNK, CHUNK), CHUNK)
        x, y, z = [
            lax.dot_general(onehot, beads_s[a, rows, :], TRANS, precision=HIGH, preferred_element_type=jnp.float32)
            for a in range(3)
        ]
        index = c * CHUNK + lax.broadcasted_iota(jnp.int32, (TPL_DEV, CHUNK), 1)
        u = coefs[0] * x + coefs[1] * y + coefs[2] * z + centre
        v = coefs[3] * x + coefs[4] * y + coefs[5] * z + centre
        u_s[:, rows] = jnp.where(index < BEADS, u, 1e4)
        v_s[:, rows] = jnp.where(index < BEADS, v, 1e4)
        return carry

    lax.fori_loop(0, BPAD // CHUNK, place, 0)

    pix = lax.broadcasted_iota(jnp.int32, (GRID, CHUNK), 0).astype(jnp.float32)

    def render(g):
        def pair(j, carry):
            for k in range(2):
                t = j * 2 + k
                acc = None
                for c in range(BPAD // CHUNK):
                    cols = pl.ds(c * CHUNK, CHUNK)
                    gu = gauss(u_s[pl.ds(g * GROUP + t, 1), cols], pix)
                    gv = gauss(v_s[pl.ds(g * GROUP + t, 1), cols], pix)
                    part_sum = lax.dot_general(gu, gv, TRANS, preferred_element_type=jnp.float32)
                    acc = part_sum if acc is None else acc + part_sum
                raw[pl.ds(pl.multiple_of(t * GRID, GRID), GRID), :] = acc
            return carry

        lax.fori_loop(0, GROUP // 2, pair, 0)
        unroll = 8

        def add(p, acc):
            for k in range(unroll):
                acc = acc + raw[pl.ds(p * unroll + k, GROUP, stride=GRID), :]
            return acc

        zero = jnp.zeros((GROUP, GRID), jnp.float32)
        total = lax.fori_loop(0, GRID // unroll, add, zero)
        mean = jnp.broadcast_to(jnp.sum(total, axis=1, keepdims=True) * (1.0 / PIX), (GROUP, GRID))

        def square(p, acc):
            for k in range(unroll):
                x = raw[pl.ds(p * unroll + k, GROUP, stride=GRID), :] - mean
                acc = acc + x * x
            return acc

        spread = lax.fori_loop(0, GRID // unroll, square, zero)
        var = jnp.sum(spread, axis=1, keepdims=True) * (1.0 / PIX)
        scale = jnp.broadcast_to(lax.rsqrt(var + 1e-05), (GROUP, GRID))
        rows = pl.ds(pl.multiple_of(r * GROUP, GROUP), GROUP)

        def put(p, carry):
            for k in range(unroll):
                x = (raw[pl.ds(p * unroll + k, GROUP, stride=GRID), :] - mean) * scale
                cols = pl.ds(pl.multiple_of((p * unroll + k) * GRID, GRID), GRID)
                tpl[g, rows, cols] = x.astype(jnp.bfloat16)
            return carry

        lax.fori_loop(0, GRID // unroll, put, 0)

    routes = [
        (r, FULL_B, part),
        (r, FULL_B, up),
        (r, FULL_B, down),
        (r, FULL_C, up),
        (r, FULL_C, down),
        (r, FULL_C, part),
        (part, FULL_B, up),
        (part, FULL_B, down),
        (down, B0, up),
        (up, B1, down),
        (down, C0, up),
        (down, FULL_C, part),
        (up, C1, down),
        (up, FULL_C, part),
        (down_part, B0, up),
        (up_part, B1, down),
        (far, C0, part),
        (far, C1, part),
    ]

    def copy_of(g, k):
        source, (start, size), target = routes[k]
        piece = tpl.at[g, pl.ds(pl.multiple_of(source * GROUP, GROUP), GROUP), pl.ds(start, size)]
        return pltpu.make_async_remote_copy(
            src_ref=piece,
            dst_ref=piece,
            send_sem=send_sem.at[g, k],
            recv_sem=recv_sem.at[g, k],
            device_id=(target, o),
            device_id_type=MESH,
        )

    def send(g, *kinds):
        for k in kinds:
            copy_of(g, k).start()

    def arrive(g, *kinds):
        for k in kinds:
            copy_of(g, k).wait_recv()

    def own(g):
        send(g, 0, 1, 2, 3, 4, 5)

    def level1(g):
        arrive(g, 0, 1, 2)
        send(g, 6, 7, 8, 9)
        arrive(g, 3, 4)
        send(g, 10, 12, 11, 13)

    def level2(g):
        arrive(g, 6, 7)
        send(g, 14, 15)
        arrive(g, 10, 12)
        send(g, 16, 17)

    def last(g):
        arrive(g, 5, 8, 9, 11, 13, 14, 15, 16, 17)

    prior_row = prior[...]
    log_prior = jnp.log(prior_row) - jnp.log(jnp.sum(prior_row, axis=1, keepdims=True))
    lane_k = lax.broadcasted_iota(jnp.int32, (N_IMG * GROUP, K), 1).astype(jnp.float32)

    def is_conf(g):
        pieces = [confb[n * TPL_DEV + g * GROUP : n * TPL_DEV + (g + 1) * GROUP, :] for n in range(N_IMG)]
        return jnp.concatenate(pieces, axis=0) == lane_k

    def score(g):
        def body(c, acc):
            cols = pl.ds(pl.multiple_of(c * SCORE_CHUNK, SCORE_CHUNK), SCORE_CHUNK)
            return acc + lax.dot_general(
                tpl[g, :, cols], img_s[:, cols], TRANS, preferred_element_type=jnp.float32
            )

        acc = lax.fori_loop(
            0, PIX // SCORE_CHUNK, body, jnp.zeros((N_IMG * GROUP, IMG_DEV), jnp.float32)
        )
        bias = jnp.sum(jnp.where(is_conf(g), log_prior, 0.0), axis=1, keepdims=True)
        lt[g] = acc * prec[...] + bias

    render(0)
    pl.semaphore_wait(barrier, N_IMG + N_ORI - 2)
    own(0)
    render(1)
    level1(0)
    own(1)
    render(2)
    level2(0)
    level1(1)
    own(2)
    image_copy.wait()
    last(0)
    score(0)
    level2(1)
    level1(2)
    last(1)
    score(1)
    level2(2)
    last(2)
    score(2)

    logits = lt[...].reshape(NGROUP * N_IMG * GROUP, IMG_DEV)
    top = jnp.max(logits, axis=0, keepdims=True)
    stat[o, :, :IMG_DEV] = top
    stat[o, :, IMG_DEV:] = jnp.sum(jnp.exp(logits - top), axis=0, keepdims=True)

    def exchange(buf, me, n, send_sems, recv_sems, device):
        copies = [
            pltpu.make_async_remote_copy(
                src_ref=buf.at[me],
                dst_ref=buf.at[me],
                send_sem=send_sems.at[j],
                recv_sem=recv_sems.at[j],
                device_id=device((me + j) % n),
                device_id_type=MESH,
            )
            for j in range(1, n)
        ]
        for copy in copies:
            copy.start()
        for copy in copies:
            copy.wait_recv()
        return copies

    pending = exchange(stat, o, N_ORI, ssend, srecv, lambda d: (r, d))
    tops = [stat[n, :, :IMG_DEV] for n in range(N_ORI)]
    peak = functools.reduce(jnp.maximum, tops)
    total = functools.reduce(
        jnp.add, [stat[n, :, IMG_DEV:] * jnp.exp(tops[n] - peak) for n in range(N_ORI)]
    )
    evidence = peak + jnp.log(total)
    out_e[...] = evidence

    partial = jnp.zeros((1, K), jnp.float32)
    for g in range(NGROUP):
        mass = jnp.sum(jnp.exp(lt[g] - evidence), axis=1, keepdims=True)
        partial = partial + jnp.sum(jnp.where(is_conf(g), mass, 0.0), axis=0, keepdims=True)
    mass_a[r] = partial
    pending += exchange(mass_a, r, N_IMG, asend, arecv, lambda d: (d, o))
    mass_b[o] = functools.reduce(jnp.add, [mass_a[n] for n in range(N_IMG)])
    pending += exchange(mass_b, o, N_ORI, bsend, brecv, lambda d: (r, d))
    totals = functools.reduce(jnp.add, [mass_b[n] for n in range(N_ORI)])
    out_w[...] = K * totals / (IMG_DEV * N_IMG)

    for copy in pending:
        copy.wait_send()
    for g in range(NGROUP):
        for k in range(N_KIND):
            copy_of(g, k).wait_send()


def local(
    images, noise_precision, prior_weight, bead_coords, euler_angles, template_conf, template_orient
):
    vmem = pl.BlockSpec(memory_space=pltpu.VMEM)
    anywhere = pl.BlockSpec(memory_space=pl.ANY)
    f32 = jnp.float32
    dma = pltpu.SemaphoreType.DMA
    weights, evidence = pl.pallas_call(
        kernel,
        out_shape=(jax.ShapeDtypeStruct((1, K), f32), jax.ShapeDtypeStruct((1, IMG_DEV), f32)),
        in_specs=[anywhere, vmem, vmem, anywhere, pl.BlockSpec(memory_space=pltpu.SMEM), vmem, vmem],
        out_specs=(vmem, vmem),
        scratch_shapes=[
            pltpu.VMEM((IMG_DEV, PIX), jnp.bfloat16),
            pltpu.VMEM((NGROUP, N_IMG * GROUP, PIX), jnp.bfloat16),
            pltpu.VMEM((3, BPAD, K), f32),
            pltpu.VMEM((TPL_DEV, BPAD), f32),
            pltpu.VMEM((TPL_DEV, BPAD), f32),
            pltpu.VMEM((GROUP * GRID, GRID), f32),
            pltpu.VMEM((NGROUP, N_IMG * GROUP, IMG_DEV), f32),
            pltpu.VMEM((N_IMG * TPL_DEV, K), f32),
            pltpu.VMEM((N_IMG * TPL_DEV, K), f32),
            pltpu.VMEM((N_ORI, 1, 2 * IMG_DEV), f32),
            pltpu.VMEM((N_IMG, 1, K), f32),
            pltpu.VMEM((N_ORI, 1, K), f32),
            dma((4,)),
            dma((NGROUP, N_KIND)),
            dma((NGROUP, N_KIND)),
            dma((N_ORI,)),
            dma((N_ORI,)),
            dma((N_IMG,)),
            dma((N_IMG,)),
            dma((N_ORI,)),
            dma((N_ORI,)),
        ],
        compiler_params=pltpu.CompilerParams(
            collective_id=0, has_side_effects=True, vmem_limit_bytes=62 << 20
        ),
    )(
        images,
        noise_precision.reshape(1, IMG_DEV),
        prior_weight.reshape(1, K),
        jnp.transpose(bead_coords, (1, 2, 0)),
        rotation_rows(euler_angles),
        template_conf.reshape(1, -1),
        template_orient.reshape(1, -1),
    )
    return (weights.reshape(K), evidence.reshape(IMG_DEV))


def solution(mesh):
    placed = (P("img", None), P("img"), P(), P(), P(None, "ori"), P("ori"), P("ori"))
    return jax.shard_map(
        local, mesh=mesh, in_specs=placed, out_specs=(P(), P("img")), check_vma=False
    )
```

time: 553 us -> 138 us (0.25)
  waiting for transfers between devices: 248 us -> 0 us
  blocking collectives: 135 us -> 0 us
  Pallas kernels: 0 us -> 129 us
  matrix products: 89.4 us -> 0 us
  local copies, waits for them, and re-layouts: 55 us -> 5.51 us
  between operations: 14.8 us -> 0.64 us
  other arithmetic: 9.07 us -> 2.12 us
    all_gather x1 -> x0, waiting for transfers between devices: 248 us -> none  [local(): lax.all_gather(rendered, 'img', axis=0, tiled=True)]
    pallas_call x0 -> x1, Pallas kernels: none -> 129 us  [local(): pl.pallas_call(kernel, out_shape=(jax.ShapeDtypeStruct((1, K), f32), jax....]
    psum x2 -> x0, blocking collectives: 102 us -> none  [the longest x1 64.2 us: local(): totals = lax.psum(conf_mass, ('img', 'ori'))]
    dot_general x16 -> x0, matrix products: 89.4 us -> none  [the longest x12 71.3 us: render(): jnp.einsum('nbp,nbq->npq', gauss_u, gauss_v, preferred_element_type=jnp.f...]
    gather x12 -> x0, local copies, waits for them, and re-layouts: 41.4 us -> none  [local(): bead_coords[item[0]]]
    pmax x1 -> x0, blocking collectives: 33.4 us -> none  [local(): global_top = lax.pmax(row_top, 'ori')]
    while x1 -> x0, local copies, waits for them, and re-layouts: 7.35 us -> none  [local(): lax.map(lambda item: render(bead_coords[item[0]], item[1]), (conf_groups,...]
  transfers between devices with their start and end apart: 1 -> 0, of which waited for: 1 -> 0; matrix products, arithmetic and copies ran while one was open for 0% -> 0% of each run, Pallas kernels for 0% -> 0%
where the time goes in v1:
time: 138 us
  Pallas kernels  129 us (93%)
  local copies, waits for them, and re-layouts  5.51 us (4%)
  other arithmetic  2.12 us (2%)
    pallas_call x1, Pallas kernels, local(): pl.pallas_call(kernel, out_shape=(jax.ShapeDtypeStruct((1, K), f32), jax....  129 us

profile of v1, /device:TPU:1, one launch (start us, length us, event | category | flops | bytes accessed | tf_op | source)
XLA Modules:
  0.0 137.6 jit_solution(11546200190374165302)
XLA Ops:
  0.6 0.9 fusion
  1.5 0.6 stack.2.coef
  2.1 1.2 reshape.22.prec
  3.3 1.3 reshape.24.conf
  4.6 1.2 reshape.25.orient
  5.9 129.3 %shard_map.86 = (f32[1,128]{1,0:T(1,128)}, f32[1,384]{1,0:T(1,128)}) custom-call(bf16[384,16384]{1,0:T(8,128)(2,1)} %images.1, f32[1,384]{1,0:T(1,128)} %reshape.22.prec, f32[1,128]{1,0:T(1,128)} %bitcast.4, f32[3,3000,128]{2,1,0:T(8,128)} %bitcast.3, f32[6,4]{1,0:T(8,128)} %stack.2.coef, s32[1,384]{1,0:T(1,128)} %reshape.24.conf, s32[1,384]{1,0:T(1,128)} %reshape.25.orient), custom_call_target="tpu_custom_call" | custom-call | tf_op jit(solution)/shard_map/pallas_call | solution.py:326
  135.2 1.3 reduce
  136.4 1.1 copy.10
